TPU v7x, 32 devices: a whole 2x2x4 slice. The times are simulated.
32 devices in a mesh: groups: 2 (over x), seq: 16 (over z, y, core).
Axes of the slice: x: 2, y: 2, z: 4, core: 2. Of those that a mesh axis runs over, the one named last changes fastest.
Arguments:
- queries: bfloat16 [4096, 8192], P(('groups', 'seq')), parts along dimension 0, may hold values from -4.5 to 4.5
- keyvalue: bfloat16 [4096, 2048], P(('groups', 'seq')), parts along dimension 0, may hold values from -4.5 to 4.5
- doc_ids: int32 [4096], P(('groups', 'seq')), parts along dimension 0, may hold values from 0 to 7, never falling along the last dimension, each value on 1 to 512 neighbouring positions
- owner_tiles: int32 [32, 2], P(('groups', 'seq')), parts along dimension 0, may hold values from 0 to 15, as said below
- tile_counts: int32 [32], P(('groups', 'seq')), parts along dimension 0, may hold values from 0 to 2, as said below
Outputs:
- owned: bfloat16 [8192, 8192], P(('groups', 'seq')), parts along dimension 0
There are 2 independent parts, one for each index of `groups`. A program takes and returns all parts, laid end to end along the dimension named above; each array names one. Nothing has to cross between parts.
Inputs may be any that keep to these rules, and one draw needn't show every extreme that they name: `owner_tiles`: over the slots below each owner's count, every tile 0 to 15 is listed exactly once; the other slots hold 0. Tile t is listed either by its holder, the owner o with o * 128 <= t * 128 < (o + 1) * 128, or by the holder's partner, the owner whose index differs from the holder's by half the number of owners. `tile_counts`: the counts sum to 16; each is 0, 1 or 2, some owner has 2, and an owner has 2 exactly when its partner has 0.
All inputs are finite; a program needn't handle non-finite values.
Results may differ from a plain program's by a relative error of at most 0.0034.
Values may be sent and summed in bfloat16 or wider, within the bound.
A program may use at most 64 MiB of HBM per device.

v0:
```python
import jax
import jax.numpy as jnp
from jax import lax
from jax.sharding import PartitionSpec as P

QUERY_HEADS = 64
KEY_VALUE_HEADS = 8
HEAD_WIDTH = 128
TILE = 128
DOCUMENT_LIMIT = 512


def from_behind(shard, axis, by):
    count = lax.axis_size(axis)
    pairs = [(i, i + by) for i in range(count) if 0 <= i + by < count]
    return lax.ppermute(shard, axis, pairs)


def attend(queries, keys, value_rows, allowed):
    scale = queries.shape[-1] ** (-0.5)
    scores = jnp.einsum("rhgd,khd->hgrk", queries, keys, preferred_element_type=jnp.float32) * scale
    scores = jnp.where(allowed[None, None], scores, -jnp.inf)
    row_top = jnp.max(scores, axis=3, keepdims=True)
    exponent = jnp.exp(scores - row_top)
    totals = jnp.sum(exponent, axis=3, keepdims=True)
    weights = exponent.astype(jnp.bfloat16)
    mixed_rows = jnp.einsum(
        "hgrk,khd->rhgd", weights, value_rows, preferred_element_type=jnp.float32
    )
    return (mixed_rows / jnp.transpose(totals, (2, 0, 1, 3))).astype(jnp.bfloat16)


def deliver_owners(head_rows, all_lists, owner_tiles, seq_count, width):
    slots_dev = owner_tiles.shape[1]
    slot_rows = slots_dev * TILE
    tile_rows = jnp.arange(TILE, dtype=jnp.int32)
    row_index = jnp.transpose(all_lists)[:, None, :] * TILE + tile_rows[None, :, None]
    send_rows = jnp.take(head_rows, row_index.reshape(slot_rows, seq_count), axis=0)
    received = lax.all_to_all(send_rows, "seq", split_axis=1, concat_axis=1, tiled=True)
    return received.reshape(slot_rows, width)


def local(queries, keyvalue, doc_ids, owner_tiles, tile_counts):
    seq_count = lax.axis_size("seq")
    token_per_holder = queries.shape[0]
    width = queries.shape[1]
    head_share = QUERY_HEADS // seq_count
    group_width = QUERY_HEADS // KEY_VALUE_HEADS
    head_cols = head_share * HEAD_WIDTH
    slots_dev = owner_tiles.shape[1]
    reach_devs = (DOCUMENT_LIMIT - 1) // token_per_holder + 1
    doc_marks = doc_ids + 1
    kv_parts = [keyvalue]
    mark_parts = [doc_marks]
    for shift_by in range(1, reach_devs + 1):
        far_kv, far_marks = from_behind((keyvalue, doc_marks), "seq", shift_by)
        kv_parts.insert(0, far_kv)
        mark_parts.insert(0, far_marks)
    kv_near = jnp.concatenate(kv_parts, axis=0)
    near_marks = jnp.concatenate(mark_parts, axis=0)
    near_rows = kv_near.shape[0]
    keyvalue_grouped = kv_near.reshape(near_rows, KEY_VALUE_HEADS, 2, HEAD_WIDTH)
    q_place = jnp.arange(token_per_holder, dtype=jnp.int32) + reach_devs * token_per_holder
    k_place = jnp.arange(near_rows, dtype=jnp.int32)
    allowed = (doc_marks[:, None] == near_marks[None, :]) & (k_place[None, :] <= q_place[:, None])
    local_out = attend(
        queries.reshape(token_per_holder, KEY_VALUE_HEADS, group_width, HEAD_WIDTH),
        keyvalue_grouped[:, :, 0],
        keyvalue_grouped[:, :, 1],
        allowed,
    )
    local_out = local_out.reshape(token_per_holder, width)
    all_lists = lax.all_gather(owner_tiles, "seq", axis=0, tiled=True)
    out_send = local_out.reshape(token_per_holder, seq_count, head_cols)
    head_rows = lax.all_to_all(out_send, "seq", split_axis=1, concat_axis=0, tiled=True).reshape(
        token_per_holder * seq_count, head_cols
    )
    owned = deliver_owners(head_rows, all_lists, owner_tiles, seq_count, width)
    live = jnp.repeat(jnp.arange(slots_dev, dtype=jnp.int32) < tile_counts[0], TILE)
    return jnp.where(live[:, None], owned, jnp.zeros((), jnp.bfloat16))


def solution(mesh):
    placed = (
        P(("groups", "seq"), None),
        P(("groups", "seq"), None),
        P(("groups", "seq")),
        P(("groups", "seq"), None),
        P(("groups", "seq")),
    )
    return jax.shard_map(
        local, mesh=mesh, in_specs=placed, out_specs=P(("groups", "seq"), None), check_vma=False
    )
```

profile of v0, /device:TPU:15, one launch (start us, length us, event | category | flops | bytes accessed | tf_op | source)
XLA Modules:
  0.0 285.1 jit_solution(12777522837619255446)
XLA Ops:
  0.0 0.7 broadcast_add_fusion
  0.7 3.2 %collective-permute-start.4 = (s32[128]{0:T(128)S(1)}, s32[128]{0:T(128)S(1)}, u32[]{:S(2)}, u32[]{:S(2)}) collective-permute-start(s32[128]{0:T(128)S(1)} %broadcast_add_fusion), channel_id=1, source_target_pairs={{0,4},{1,5},{2,6},{3,7},{4,8},{5,9},{6,10},{7,11},{8,12},{9,13},{1... | collective-permute-start | bytes 1544 | tf_op jit(solution)/shard_map/ppermute | solution.py:16
  3.9 4.0 %collective-permute-start.5 = (s32[128]{0:T(128)S(1)}, s32[128]{0:T(128)S(1)}, u32[]{:S(2)}, u32[]{:S(2)}) collective-permute-start(s32[128]{0:T(128)S(1)} %broadcast_add_fusion), channel_id=1, source_target_pairs={{0,3},{1,4},{2,5},{3,6},{4,7},{5,8},{6,9},{7,10},{8,11},{9,12},{10... | collective-permute-start | bytes 1544 | tf_op jit(solution)/shard_map/ppermute | solution.py:16
  8.0 1.9 collective-permute-start.6
  9.9 3.4 %collective-permute-start.7 = (s32[128]{0:T(128)S(1)}, s32[128]{0:T(128)S(1)}, u32[]{:S(2)}, u32[]{:S(2)}) collective-permute-start(s32[128]{0:T(128)S(1)} %broadcast_add_fusion), channel_id=1, source_target_pairs={{0,1},{1,2},{2,3},{3,4},{4,5},{5,6},{6,7},{7,8},{8,9},{9,10},{10,1... | collective-permute-start | bytes 1544 | tf_op jit(solution)/shard_map/ppermute | solution.py:16
  13.3 1.3 copy.52
  14.6 1.9 collective-permute-start
  16.6 2.2 copy.71
  18.8 1.9 collective-permute-start.1
  20.7 1.9 collective-permute-start.2
  22.7 2.2 collective-permute-start.3
  24.9 0.2 fusion.11
  25.1 5.3 %collective-permute-done = bf16[128,2048]{0,1:T(8,128)(2,1)S(1)} collective-permute-done((bf16[128,2048]{0,1:T(8,128)(2,1)S(1)}, bf16[128,2048]{0,1:T(8,128)(2,1)S(1)}, u32[]{:S(2)}, u32[]{:S(2)}) %collective-permute-start) | collective-permute-done | bytes 524320 | tf_op jit(solution)/shard_map/ppermute | solution.py:16
  30.5 9.0 %collective-permute-done.1 = bf16[128,2048]{0,1:T(8,128)(2,1)S(1)} collective-permute-done((bf16[128,2048]{0,1:T(8,128)(2,1)S(1)}, bf16[128,2048]{0,1:T(8,128)(2,1)S(1)}, u32[]{:S(2)}, u32[]{:S(2)}) %collective-permute-start.1) | collective-permute-done | bytes 524320 | tf_op jit(solution)/shard_map/ppermute | solution.py:16
  39.6 10.8 %collective-permute-done.2 = bf16[128,2048]{0,1:T(8,128)(2,1)S(1)} collective-permute-done((bf16[128,2048]{0,1:T(8,128)(2,1)S(1)}, bf16[128,2048]{0,1:T(8,128)(2,1)S(1)}, u32[]{:S(2)}, u32[]{:S(2)}) %collective-permute-start.2) | collective-permute-done | bytes 524320 | tf_op jit(solution)/shard_map/ppermute | solution.py:16
  50.6 5.5 %collective-permute-done.3 = bf16[128,2048]{0,1:T(8,128)(2,1)S(1)} collective-permute-done((bf16[128,2048]{0,1:T(8,128)(2,1)S(1)}, bf16[128,2048]{0,1:T(8,128)(2,1)S(1)}, u32[]{:S(2)}, u32[]{:S(2)}) %collective-permute-start.3) | collective-permute-done | bytes 524320 | tf_op jit(solution)/shard_map/ppermute | solution.py:16
  56.2 0.1 constant_dynamic-update-slice_fusion
  56.4 1.5 copy-done.1
  57.8 5.9 %fusion.2 = (f32[8,8,128]{2,1,0:T(8,128)S(1)}, f32[8,640,128,8]{2,1,3,0:T(8,128)S(1)}) fusion(pred[128,640]{0,1:T(8,128)(4,1)S(1)} %fusion.11, bf16[128,8,8,128]{3,2,1,0:T(8,128)(2,1)S(1)} %bitcast.69, bf16[640,8,2,128]{0,3,2,1:T(8,128)(2,1)} %bitcast.71), kind=kOutput, calls=%fused_computation.5 | convolution fusion | flops 1357897728 | bytes 24494080 | tf_op jit(solution)/shard_map/rhgd,khd->hgrk/dot_general | solution.py:21
  63.8 5.7 %fusion = f32[8,8,128]{2,1,0:T(8,128)} fusion(f32[8,640,128,8]{2,1,3,0:T(8,128)S(1)} %get-tuple-element.6, f32[8,8,128]{2,1,0:T(8,128)S(1)} %get-tuple-element.5, pred[128,640]{0,1:T(8,128)(4,1)S(1)} %fusion.11), kind=kLoop, calls=%fused_computation.3 | loop fusion | flops 20963328 | bytes 21118976 | tf_op jit(solution)/shard_map/reduce_sum | solution.py:25
  69.5 7.8 %fusion.6 = bf16[128,8,8,128]{0,3,2,1:T(8,128)(2,1)} fusion(f32[8,640,128,8]{2,1,3,0:T(8,128)S(1)} %get-tuple-element.6, f32[8,8,128]{2,1,0:T(8,128)S(1)} %get-tuple-element.5, pred[128,640]{0,1:T(8,128)(4,1)} %copy-done.2, f32[128,8,8]{0,2,1:T(8,128)} %bitcast.76, bf16[640,8,2,128]{0,3,2,1:T(8,128)(2,1)} %bitcast.72), kind=kOutput, calls=%fused_computation.10 | convolution fusion | flops 1365245952 | bytes 24526848 | tf_op jit(solution)/shard_map/hgrk,khd->rhgd/dot_general | solution.py:27
  77.2 6.8 %all-to-all-start = ((bf16[128,16,512]{0,2,1:T(8,128)(2,1)}), bf16[128,16,512]{0,2,1:T(8,128)(2,1)S(1)}, u32[]{:S(2)}, u32[]{:S(2)}) async-start(bf16[128,16,512]{0,2,1:T(8,128)(2,1)} %bitcast.74), calls=%async_computation | async-start | bytes 4194304 | tf_op jit(solution)/shard_map/all_to_all | solution.py:75
  84.1 56.9 %all-gather = s32[16,1,2]{2,1,0:T(1,128)S(1)} all-gather(s32[1,1,2]{2,1,0:T(1,128)S(1)} %bitcast.77), channel_id=1, replica_groups=mesh['groups'=2,'seq'=16] {'seq'}, dimensions={0}, use_global_device_ids=true | all-gather | bytes 136 | tf_op jit(solution)/shard_map/all_gather | solution.py:73
  141.4 1.3 copy-done
  142.7 2.9 %copy.61 = bf16[16,128,1,512]{3,1,0,2:T(8,128)(2,1)S(1)} copy(bf16[16,128,1,512]{1,3,0,2:T(8,128)(2,1)} %bitcast.70) | data formatting | bytes 4194304 | tf_op jit(solution)/shard_map/all_to_all | solution.py:75
  145.5 17.3 %gather_fusion = bf16[4096,512]{1,0:T(8,128)(2,1)} fusion(bf16[2048,512]{1,0:T(8,128)(2,1)S(1)} %bitcast.67, s32[4096]{0:T(1024)S(1)} %broadcast_clamp_fusion), kind=kCustom, calls=%fused_computation | custom fusion | bytes 8404992 | tf_op jit(solution)/shard_map/jit(_take)/gather | solution.py:38
  162.9 7.5 %copy_select_fusion = bf16[256,16,512]{2,0,1:T(8,128)(2,1)} fusion(bf16[256,16,512]{2,1,0:T(8,128)(2,1)} %bitcast.68, pred[256,16]{0,1:T(8,128)(4,1)S(1)} %compare_and_fusion), kind=kLoop, calls=%fused_computation.11 | loop fusion | flops 2097152 | bytes 8392704 | tf_op jit(solution)/shard_map/jit(_take)/select_n | solution.py:38
  170.4 4.9 %all-to-all-start.1 = ((bf16[256,16,512]{2,0,1:T(8,128)(2,1)}), bf16[256,16,512]{2,0,1:T(8,128)(2,1)}, u32[]{:S(2)}, u32[]{:S(2)}) async-start(bf16[256,16,512]{2,0,1:T(8,128)(2,1)} %copy_select_fusion), calls=%async_computation.1 | async-start | bytes 8388608 | tf_op jit(solution)/shard_map/all_to_all | solution.py:39
  176.0 92.0 %all-to-all-done.1 = bf16[256,16,512]{2,0,1:T(8,128)(2,1)} async-done(((bf16[256,16,512]{2,0,1:T(8,128)(2,1)}), bf16[256,16,512]{2,0,1:T(8,128)(2,1)}, u32[]{:S(2)}, u32[]{:S(2)}) %all-to-all-start.1) | async-done | bytes 4194336 | tf_op jit(solution)/shard_map/all_to_all | solution.py:39
  268.0 6.4 %copy.63 = bf16[256,16,512]{0,2,1:T(8,128)(2,1)} copy(bf16[256,16,512]{2,0,1:T(8,128)(2,1)} %all-to-all-done.1) | data formatting | bytes 8388608 | tf_op jit(solution)/shard_map/all_to_all | solution.py:39
  274.4 4.4 %bitcast_select_fusion.1 = bf16[256,8192]{0,1:T(8,128)(2,1)} fusion(bf16[256,16,512]{0,2,1:T(8,128)(2,1)} %copy.63, pred[256]{0:T(512)(128)(4,1)S(1)} %broadcast_bitcast_fusion), kind=kLoop, calls=%fused_computation.8 | loop fusion | flops 2097152 | bytes 8388864 | tf_op jit(solution)/shard_map/jit(_where)/select_n | solution.py:80
  278.8 6.3 %copy.64 = bf16[256,8192]{1,0:T(8,128)(2,1)} copy(bf16[256,8192]{0,1:T(8,128)(2,1)} %bitcast_select_fusion.1) | data formatting | bytes 8388608 | tf_op jit(solution)/shard_map/jit(_where)/select_n | solution.py:80
  (35 shorter events, 1.0 us)
Async XLA Ops:
  0.0 24.9 %copy-start.4 = (s32[128]{0:T(128)S(1)}, s32[128]{0:T(128)}, u32[]{:S(2)}) copy-start(s32[128]{0:T(128)} %param.7) | copy-start | bytes 1540
  0.7 18.0 %collective-permute-start.4 = (s32[128]{0:T(128)S(1)}, s32[128]{0:T(128)S(1)}, u32[]{:S(2)}, u32[]{:S(2)}) collective-permute-start(s32[128]{0:T(128)S(1)} %broadcast_add_fusion), channel_id=1, source_target_pairs={{0,4},{1,5},{2,6},{3,7},{4,8},{5,9},{6,10},{7,11},{8,12},{9,13},{1... | collective-permute-start | bytes 1544 | tf_op jit(solution)/shard_map/ppermute | solution.py:16
  3.9 16.8 %collective-permute-start.5 = (s32[128]{0:T(128)S(1)}, s32[128]{0:T(128)S(1)}, u32[]{:S(2)}, u32[]{:S(2)}) collective-permute-start(s32[128]{0:T(128)S(1)} %broadcast_add_fusion), channel_id=1, source_target_pairs={{0,3},{1,4},{2,5},{3,6},{4,7},{5,8},{6,9},{7,10},{8,11},{9,12},{10... | collective-permute-start | bytes 1544 | tf_op jit(solution)/shard_map/ppermute | solution.py:16
  8.0 14.7 %collective-permute-start.6 = (s32[128]{0:T(128)S(1)}, s32[128]{0:T(128)S(1)}, u32[]{:S(2)}, u32[]{:S(2)}) collective-permute-start(s32[128]{0:T(128)S(1)} %broadcast_add_fusion), channel_id=1, source_target_pairs={{0,2},{1,3},{2,4},{3,5},{4,6},{5,7},{6,8},{7,9},{8,10},{9,11},{10,... | collective-permute-start | bytes 1544 | tf_op jit(solution)/shard_map/ppermute | solution.py:16
  9.9 15.0 %collective-permute-start.7 = (s32[128]{0:T(128)S(1)}, s32[128]{0:T(128)S(1)}, u32[]{:S(2)}, u32[]{:S(2)}) collective-permute-start(s32[128]{0:T(128)S(1)} %broadcast_add_fusion), channel_id=1, source_target_pairs={{0,1},{1,2},{2,3},{3,4},{4,5},{5,6},{6,7},{7,8},{8,9},{9,10},{10,1... | collective-permute-start | bytes 1544 | tf_op jit(solution)/shard_map/ppermute | solution.py:16
  14.6 15.8 %collective-permute-start = (bf16[128,2048]{0,1:T(8,128)(2,1)S(1)}, bf16[128,2048]{0,1:T(8,128)(2,1)S(1)}, u32[]{:S(2)}, u32[]{:S(2)}) collective-permute-start(bf16[128,2048]{0,1:T(8,128)(2,1)S(1)} %copy.52), channel_id=1, source_target_pairs={{0,4},{1,5},{2,6},{3,7},{4,8},{5,9},{6,10},{7,11},{8,12},{9,13},{1... | collective-permute-start | bytes 1572872 | tf_op jit(solution)/shard_map/ppermute | solution.py:16
  18.8 20.7 %collective-permute-start.1 = (bf16[128,2048]{0,1:T(8,128)(2,1)S(1)}, bf16[128,2048]{0,1:T(8,128)(2,1)S(1)}, u32[]{:S(2)}, u32[]{:S(2)}) collective-permute-start(bf16[128,2048]{0,1:T(8,128)(2,1)S(1)} %copy.52), channel_id=1, source_target_pairs={{0,3},{1,4},{2,5},{3,6},{4,7},{5,8},{6,9},{7,10},{8,11},{9,12},{10... | collective-permute-start | bytes 1572872 | tf_op jit(solution)/shard_map/ppermute | solution.py:16
  20.7 29.8 %collective-permute-start.2 = (bf16[128,2048]{0,1:T(8,128)(2,1)S(1)}, bf16[128,2048]{0,1:T(8,128)(2,1)S(1)}, u32[]{:S(2)}, u32[]{:S(2)}) collective-permute-start(bf16[128,2048]{0,1:T(8,128)(2,1)S(1)} %copy.52), channel_id=1, source_target_pairs={{0,2},{1,3},{2,4},{3,5},{4,6},{5,7},{6,8},{7,9},{8,10},{9,11},{10,... | collective-permute-start | bytes 1572872 | tf_op jit(solution)/shard_map/ppermute | solution.py:16
  22.7 33.4 %collective-permute-start.3 = (bf16[128,2048]{0,1:T(8,128)(2,1)S(1)}, bf16[128,2048]{0,1:T(8,128)(2,1)S(1)}, u32[]{:S(2)}, u32[]{:S(2)}) collective-permute-start(bf16[128,2048]{0,1:T(8,128)(2,1)S(1)} %copy.52), channel_id=1, source_target_pairs={{0,1},{1,2},{2,3},{3,4},{4,5},{5,6},{6,7},{7,8},{8,9},{9,10},{10,1... | collective-permute-start | bytes 1572872 | tf_op jit(solution)/shard_map/ppermute | solution.py:16
  25.1 38.7 %copy-start.2 = (pred[128,640]{0,1:T(8,128)(4,1)}, pred[128,640]{0,1:T(8,128)(4,1)S(1)}, u32[]{:S(2)}) copy-start(pred[128,640]{0,1:T(8,128)(4,1)S(1)} %fusion.11) | copy-start | bytes 245764
  56.3 1.5 copy-start.1
  77.2 6.8 %copy-start.3 = (s32[1,2]{1,0:T(1,128)S(1)}, s32[1,2]{1,0:T(1,128)}, u32[]{:S(2)}) copy-start(s32[1,2]{1,0:T(1,128)} %param.8) | copy-start | bytes 28
  77.2 64.1 %all-to-all-start = ((bf16[128,16,512]{0,2,1:T(8,128)(2,1)}), bf16[128,16,512]{0,2,1:T(8,128)(2,1)S(1)}, u32[]{:S(2)}, u32[]{:S(2)}) async-start(bf16[128,16,512]{0,2,1:T(8,128)(2,1)} %bitcast.74), calls=%async_computation | async-start | bytes 4194304 | tf_op jit(solution)/shard_map/all_to_all | solution.py:75
  141.4 1.3 copy-start
  170.4 97.6 %all-to-all-start.1 = ((bf16[256,16,512]{2,0,1:T(8,128)(2,1)}), bf16[256,16,512]{2,0,1:T(8,128)(2,1)}, u32[]{:S(2)}, u32[]{:S(2)}) async-start(bf16[256,16,512]{2,0,1:T(8,128)(2,1)} %copy_select_fusion), calls=%async_computation.1 | async-start | bytes 8388608 | tf_op jit(solution)/shard_map/all_to_all | solution.py:39
where the time goes:
time: 286 us; the launch traced here: 285 us
  waiting for transfers between devices  123 us (43%)
  blocking collectives  56.9 us (20%)
  local copies, waits for them, and re-layouts  40.1 us (14%)
  starting transfers between devices  32.2 us (11%)
  other arithmetic  18.6 us (7%)
  matrix products  13.7 us (5%)
    all_to_all x1, waiting for transfers between devices, deliver_owners(): lax.all_to_all(send_rows, 'seq', split_axis=1, concat_axis=1, tiled=True)  92 us
    all_gather x1, blocking collectives, local(): all_lists = lax.all_gather(owner_tiles, 'seq', axis=0, tiled=True)  56.9 us
    ppermute x8, waiting for transfers between devices, from_behind(): return lax.ppermute(shard, axis, pairs)  30.7 us
    ppermute x8, starting transfers between devices, from_behind(): return lax.ppermute(shard, axis, pairs)  20.5 us
    gather x1, local copies, waits for them, and re-layouts, deliver_owners(): jnp.take(head_rows, row_index.reshape(slot_rows, seq_count), axis=0)  17.3 us
    dot_general x1, matrix products, attend(): jnp.einsum('hgrk,khd->rhgd', weights, value_rows, preferred_element_type=...  7.78 us
    select_n x2, other arithmetic, deliver_owners(): jnp.take(head_rows, row_index.reshape(slot_rows, seq_count), axis=0)  7.62 us
    all_to_all x1, starting transfers between devices, local(): lax.all_to_all(out_send, 'seq', split_axis=1, concat_axis=0, tiled=True)  6.8 us
  transfers between devices with their start and end apart: 10, of which 5 were waited for; matrix products, arithmetic and copies ran while one was open for 2% of the time, Pallas kernels for 0%

commit v1 on v0

--- a/solution.py
+++ b/solution.py
@@ -30,23 +30,11 @@
     return (mixed_rows / jnp.transpose(totals, (2, 0, 1, 3))).astype(jnp.bfloat16)
 
 
-def deliver_owners(head_rows, all_lists, owner_tiles, seq_count, width):
-    slots_dev = owner_tiles.shape[1]
-    slot_rows = slots_dev * TILE
-    tile_rows = jnp.arange(TILE, dtype=jnp.int32)
-    row_index = jnp.transpose(all_lists)[:, None, :] * TILE + tile_rows[None, :, None]
-    send_rows = jnp.take(head_rows, row_index.reshape(slot_rows, seq_count), axis=0)
-    received = lax.all_to_all(send_rows, "seq", split_axis=1, concat_axis=1, tiled=True)
-    return received.reshape(slot_rows, width)
-
-
 def local(queries, keyvalue, doc_ids, owner_tiles, tile_counts):
     seq_count = lax.axis_size("seq")
     token_per_holder = queries.shape[0]
     width = queries.shape[1]
-    head_share = QUERY_HEADS // seq_count
     group_width = QUERY_HEADS // KEY_VALUE_HEADS
-    head_cols = head_share * HEAD_WIDTH
     slots_dev = owner_tiles.shape[1]
     reach_devs = (DOCUMENT_LIMIT - 1) // token_per_holder + 1
     doc_marks = doc_ids + 1
@@ -70,14 +58,15 @@
         allowed,
     )
     local_out = local_out.reshape(token_per_holder, width)
-    all_lists = lax.all_gather(owner_tiles, "seq", axis=0, tiled=True)
-    out_send = local_out.reshape(token_per_holder, seq_count, head_cols)
-    head_rows = lax.all_to_all(out_send, "seq", split_axis=1, concat_axis=0, tiled=True).reshape(
-        token_per_holder * seq_count, head_cols
-    )
-    owned = deliver_owners(head_rows, all_lists, owner_tiles, seq_count, width)
-    live = jnp.repeat(jnp.arange(slots_dev, dtype=jnp.int32) < tile_counts[0], TILE)
-    return jnp.where(live[:, None], owned, jnp.zeros((), jnp.bfloat16))
+    half = seq_count // 2
+    swap = [(i, (i + half) % seq_count) for i in range(seq_count)]
+    far_out = lax.ppermute(local_out, "seq", swap)
+    me = lax.axis_index("seq")
+    live = jnp.arange(slots_dev, dtype=jnp.int32) < tile_counts[0]
+    mine = (owner_tiles[0] == me)[:, None, None]
+    owned = jnp.where(mine, local_out[None], far_out[None])
+    owned = jnp.where(live[:, None, None], owned, jnp.zeros((), jnp.bfloat16))
+    return owned.reshape(slots_dev * TILE, width)
 
 
 def solution(mesh):

time: 286 us -> 177 us (0.62)
  the two profiles are of different devices: /device:TPU:15 before, /device:TPU:0 now
where the time goes in v1:
time: 177 us
  waiting for transfers between devices  98.6 us (56%)
  starting transfers between devices  39.4 us (22%)
  matrix products  13.8 us (8%)
  local copies, waits for them, and re-layouts  12.6 us (7%)
  other arithmetic  11.4 us (6%)
    ppermute x1, waiting for transfers between devices, local(): far_out = lax.ppermute(local_out, 'seq', swap)  81.7 us
    ppermute x8, starting transfers between devices, from_behind(): return lax.ppermute(shard, axis, pairs)  24.4 us
    ppermute x8, waiting for transfers between devices, from_behind(): return lax.ppermute(shard, axis, pairs)  16.9 us
    ppermute x1, starting transfers between devices, local(): far_out = lax.ppermute(local_out, 'seq', swap)  15 us
    dot_general x1, matrix products, attend(): jnp.einsum('hgrk,khd->rhgd', weights, value_rows, preferred_element_type=...  7.77 us
    dot_general x1, matrix products, attend(): jnp.einsum('rhgd,khd->hgrk', queries, keys, preferred_element_type=jnp.fl...  5.98 us
    reduce_sum x1, other arithmetic, attend(): totals = jnp.sum(exponent, axis=3, keepdims=True)  5.67 us
    unnamed x18, local copies, waits for them, and re-layouts  5.48 us
  transfers between devices with their start and end apart: 9, of which 4 were waited for; matrix products, arithmetic and copies ran while one was open for 4% of the time, Pallas kernels for 0%

profile of v1, /device:TPU:0, one launch (start us, length us, event | category | flops | bytes accessed | tf_op | source)
XLA Modules:
  0.0 176.7 jit_solution(10426514208938888312)
XLA Ops:
  0.0 0.7 broadcast_add_fusion
  0.7 5.1 %collective-permute-start.4 = (s32[128]{0:T(128)S(1)}, s32[128]{0:T(128)S(1)}, u32[]{:S(2)}, u32[]{:S(2)}) collective-permute-start(s32[128]{0:T(128)S(1)} %broadcast_add_fusion), channel_id=1, source_target_pairs={{0,4},{1,5},{2,6},{3,7},{4,8},{5,9},{6,10},{7,11},{8,12},{9,13},{1... | collective-permute-start | bytes 1544 | tf_op jit(solution)/shard_map/ppermute | solution.py:16
  5.7 2.6 %collective-permute-start.5 = (s32[128]{0:T(128)S(1)}, s32[128]{0:T(128)S(1)}, u32[]{:S(2)}, u32[]{:S(2)}) collective-permute-start(s32[128]{0:T(128)S(1)} %broadcast_add_fusion), channel_id=1, source_target_pairs={{0,3},{1,4},{2,5},{3,6},{4,7},{5,8},{6,9},{7,10},{8,11},{9,12},{10... | collective-permute-start | bytes 1544 | tf_op jit(solution)/shard_map/ppermute | solution.py:16
  8.3 3.4 %collective-permute-start.6 = (s32[128]{0:T(128)S(1)}, s32[128]{0:T(128)S(1)}, u32[]{:S(2)}, u32[]{:S(2)}) collective-permute-start(s32[128]{0:T(128)S(1)} %broadcast_add_fusion), channel_id=1, source_target_pairs={{0,2},{1,3},{2,4},{3,5},{4,6},{5,7},{6,8},{7,9},{8,10},{9,11},{10,... | collective-permute-start | bytes 1544 | tf_op jit(solution)/shard_map/ppermute | solution.py:16
  11.8 2.6 %collective-permute-start.7 = (s32[128]{0:T(128)S(1)}, s32[128]{0:T(128)S(1)}, u32[]{:S(2)}, u32[]{:S(2)}) collective-permute-start(s32[128]{0:T(128)S(1)} %broadcast_add_fusion), channel_id=1, source_target_pairs={{0,1},{1,2},{2,3},{3,4},{4,5},{5,6},{6,7},{7,8},{8,9},{9,10},{10,1... | collective-permute-start | bytes 1544 | tf_op jit(solution)/shard_map/ppermute | solution.py:16
  14.4 1.3 copy.11
  15.7 3.5 %collective-permute-start = (bf16[128,2048]{0,1:T(8,128)(2,1)S(1)}, bf16[128,2048]{0,1:T(8,128)(2,1)S(1)}, u32[]{:S(2)}, u32[]{:S(2)}) collective-permute-start(bf16[128,2048]{0,1:T(8,128)(2,1)S(1)} %copy.11), channel_id=1, source_target_pairs={{0,4},{1,5},{2,6},{3,7},{4,8},{5,9},{6,10},{7,11},{8,12},{9,13},{1... | collective-permute-start | bytes 1572872 | tf_op jit(solution)/shard_map/ppermute | solution.py:16
  19.3 2.2 %copy.27 = bf16[16,8,64,128]{3,2,1,0:T(8,128)(2,1)S(1)} copy(bf16[16,8,64,128]{3,1,2,0:T(8,128)(2,1)} %bitcast.59) | data formatting | bytes 4194304
  21.5 3.0 %collective-permute-start.1 = (bf16[128,2048]{0,1:T(8,128)(2,1)S(1)}, bf16[128,2048]{0,1:T(8,128)(2,1)S(1)}, u32[]{:S(2)}, u32[]{:S(2)}) collective-permute-start(bf16[128,2048]{0,1:T(8,128)(2,1)S(1)} %copy.11), channel_id=1, source_target_pairs={{0,3},{1,4},{2,5},{3,6},{4,7},{5,8},{6,9},{7,10},{8,11},{9,12},{10... | collective-permute-start | bytes 1572872 | tf_op jit(solution)/shard_map/ppermute | solution.py:16
  24.5 2.8 %collective-permute-start.2 = (bf16[128,2048]{0,1:T(8,128)(2,1)S(1)}, bf16[128,2048]{0,1:T(8,128)(2,1)S(1)}, u32[]{:S(2)}, u32[]{:S(2)}) collective-permute-start(bf16[128,2048]{0,1:T(8,128)(2,1)S(1)} %copy.11), channel_id=1, source_target_pairs={{0,2},{1,3},{2,4},{3,5},{4,6},{5,7},{6,8},{7,9},{8,10},{9,11},{10,... | collective-permute-start | bytes 1572872 | tf_op jit(solution)/shard_map/ppermute | solution.py:16
  27.4 0.0 collective-permute-done.6
  27.4 1.3 collective-permute-start.3
  28.8 0.8 fusion.12
  29.6 2.0 %collective-permute-done = bf16[128,2048]{0,1:T(8,128)(2,1)S(1)} collective-permute-done((bf16[128,2048]{0,1:T(8,128)(2,1)S(1)}, bf16[128,2048]{0,1:T(8,128)(2,1)S(1)}, u32[]{:S(2)}, u32[]{:S(2)}) %collective-permute-start) | collective-permute-done | bytes 524320 | tf_op jit(solution)/shard_map/ppermute | solution.py:16
  31.5 0.1 constant_dynamic-update-slice_fusion.4
  31.6 3.8 %collective-permute-done.1 = bf16[128,2048]{0,1:T(8,128)(2,1)S(1)} collective-permute-done((bf16[128,2048]{0,1:T(8,128)(2,1)S(1)}, bf16[128,2048]{0,1:T(8,128)(2,1)S(1)}, u32[]{:S(2)}, u32[]{:S(2)}) %collective-permute-start.1) | collective-permute-done | bytes 524320 | tf_op jit(solution)/shard_map/ppermute | solution.py:16
  35.4 0.1 constant_dynamic-update-slice_fusion.3
  35.5 11.1 %collective-permute-done.2 = bf16[128,2048]{0,1:T(8,128)(2,1)S(1)} collective-permute-done((bf16[128,2048]{0,1:T(8,128)(2,1)S(1)}, bf16[128,2048]{0,1:T(8,128)(2,1)S(1)}, u32[]{:S(2)}, u32[]{:S(2)}) %collective-permute-start.2) | collective-permute-done | bytes 524320 | tf_op jit(solution)/shard_map/ppermute | solution.py:16
  46.6 0.1 constant_dynamic-update-slice_fusion.2
  46.8 0.1 constant_dynamic-update-slice_fusion.1
  46.9 0.1 constant_dynamic-update-slice_fusion
  47.0 0.0 copy-start
  47.1 1.5 copy-done
  48.5 6.0 %fusion.2 = (f32[8,8,128]{2,1,0:T(8,128)S(1)}, f32[8,640,128,8]{2,1,3,0:T(8,128)S(1)}) fusion(pred[128,640]{0,1:T(8,128)(4,1)} %fusion.12, bf16[128,8,8,128]{3,2,1,0:T(8,128)(2,1)S(1)} %bitcast.56, bf16[640,8,2,128]{0,3,2,1:T(8,128)(2,1)} %bitcast.57), kind=kOutput, calls=%fused_computation.4 | convolution fusion | flops 1357897728 | bytes 24494080 | tf_op jit(solution)/shard_map/rhgd,khd->hgrk/dot_general | solution.py:21
  54.5 5.7 %fusion = f32[8,8,128]{2,1,0:T(8,128)} fusion(f32[8,640,128,8]{2,1,3,0:T(8,128)S(1)} %get-tuple-element.6, f32[8,8,128]{2,1,0:T(8,128)S(1)} %get-tuple-element.5, pred[128,640]{0,1:T(8,128)(4,1)S(1)} %copy-done.1), kind=kLoop, calls=%fused_computation.2 | loop fusion | flops 20963328 | bytes 21118976 | tf_op jit(solution)/shard_map/reduce_sum | solution.py:25
  60.2 7.8 %fusion.7 = bf16[128,8,8,128]{0,3,2,1:T(8,128)(2,1)} fusion(f32[8,640,128,8]{2,1,3,0:T(8,128)S(1)} %get-tuple-element.6, f32[8,8,128]{2,1,0:T(8,128)S(1)} %get-tuple-element.5, pred[128,640]{0,1:T(8,128)(4,1)} %fusion.12, f32[128,8,8]{0,2,1:T(8,128)} %bitcast.62, bf16[640,8,2,128]{0,3,2,1:T(8,128)(2,1)} %bitcast.58), kind=kOutput, calls=%fused_computation.10 | convolution fusion | flops 1365245952 | bytes 24526848 | tf_op jit(solution)/shard_map/hgrk,khd->rhgd/dot_general | solution.py:27
  68.0 15.0 %collective-permute-start.8 = (bf16[128,8192]{0,1:T(8,128)(2,1)}, bf16[128,8192]{0,1:T(8,128)(2,1)}, u32[]{:S(2)}, u32[]{:S(2)}) collective-permute-start(bf16[128,8192]{0,1:T(8,128)(2,1)} %bitcast.60), channel_id=1, source_target_pairs={{0,8},{1,9},{2,10},{3,11},{4,12},{5,13},{6,14},{7,15},{8,0},{9,1},... | collective-permute-start | bytes 6291464 | tf_op jit(solution)/shard_map/ppermute | solution.py:63
  83.7 0.1 broadcast_bitcast_fusion
  83.7 2.9 %copy.20 = bf16[128,8192]{1,0:T(8,128)(2,1)S(1)} copy(bf16[128,8192]{0,1:T(8,128)(2,1)} %bitcast.61) | data formatting | bytes 4194304 | tf_op jit(solution)/shard_map/jit(_where)/broadcast_in_dim | solution.py:67
  86.7 81.7 %collective-permute-done.8 = bf16[128,8192]{0,1:T(8,128)(2,1)} collective-permute-done((bf16[128,8192]{0,1:T(8,128)(2,1)}, bf16[128,8192]{0,1:T(8,128)(2,1)}, u32[]{:S(2)}, u32[]{:S(2)}) %collective-permute-start.8) | collective-permute-done | bytes 2097184 | tf_op jit(solution)/shard_map/ppermute | solution.py:63
  168.4 4.0 %copy.21 = bf16[128,8192]{1,0:T(8,128)(2,1)} copy(bf16[128,8192]{0,1:T(8,128)(2,1)} %collective-permute-done.8) | data formatting | bytes 4194304 | tf_op jit(solution)/shard_map/ppermute | solution.py:63
  172.4 4.2 %fusion.6 = bf16[256,8192]{1,0:T(8,128)(2,1)} fusion(pred[256]{0:T(512)(128)(4,1)S(1)} %get-tuple-element.7, pred[256]{0:T(512)(128)(4,1)S(1)} %get-tuple-element.8, bf16[128,8192]{1,0:T(8,128)(2,1)} %copy.21, bf16[128,8192]{1,0:T(8,128)(2,1)S(1)} %copy.20), kind=kLoop, calls=%fused_computation.8 | loop fusion | flops 4194304 | bytes 8389120 | tf_op jit(solution)/shard_map/jit(_where)/select_n | solution.py:68
  (19 shorter events, 0.1 us)
Async XLA Ops:
  0.7 28.1 %copy-start.2 = (s32[128]{0:T(128)S(1)}, s32[128]{0:T(128)}, u32[]{:S(2)}) copy-start(s32[128]{0:T(128)} %param.7) | copy-start | bytes 1540
  0.7 20.8 %collective-permute-start.4 = (s32[128]{0:T(128)S(1)}, s32[128]{0:T(128)S(1)}, u32[]{:S(2)}, u32[]{:S(2)}) collective-permute-start(s32[128]{0:T(128)S(1)} %broadcast_add_fusion), channel_id=1, source_target_pairs={{0,4},{1,5},{2,6},{3,7},{4,8},{5,9},{6,10},{7,11},{8,12},{9,13},{1... | collective-permute-start | bytes 1544 | tf_op jit(solution)/shard_map/ppermute | solution.py:16
  5.7 18.8 %collective-permute-start.5 = (s32[128]{0:T(128)S(1)}, s32[128]{0:T(128)S(1)}, u32[]{:S(2)}, u32[]{:S(2)}) collective-permute-start(s32[128]{0:T(128)S(1)} %broadcast_add_fusion), channel_id=1, source_target_pairs={{0,3},{1,4},{2,5},{3,6},{4,7},{5,8},{6,9},{7,10},{8,11},{9,12},{10... | collective-permute-start | bytes 1544 | tf_op jit(solution)/shard_map/ppermute | solution.py:16
  8.3 19.0 %collective-permute-start.6 = (s32[128]{0:T(128)S(1)}, s32[128]{0:T(128)S(1)}, u32[]{:S(2)}, u32[]{:S(2)}) collective-permute-start(s32[128]{0:T(128)S(1)} %broadcast_add_fusion), channel_id=1, source_target_pairs={{0,2},{1,3},{2,4},{3,5},{4,6},{5,7},{6,8},{7,9},{8,10},{9,11},{10,... | collective-permute-start | bytes 1544 | tf_op jit(solution)/shard_map/ppermute | solution.py:16
  11.8 17.0 %collective-permute-start.7 = (s32[128]{0:T(128)S(1)}, s32[128]{0:T(128)S(1)}, u32[]{:S(2)}, u32[]{:S(2)}) collective-permute-start(s32[128]{0:T(128)S(1)} %broadcast_add_fusion), channel_id=1, source_target_pairs={{0,1},{1,2},{2,3},{3,4},{4,5},{5,6},{6,7},{7,8},{8,9},{9,10},{10,1... | collective-permute-start | bytes 1544 | tf_op jit(solution)/shard_map/ppermute | solution.py:16
  15.7 15.8 %collective-permute-start = (bf16[128,2048]{0,1:T(8,128)(2,1)S(1)}, bf16[128,2048]{0,1:T(8,128)(2,1)S(1)}, u32[]{:S(2)}, u32[]{:S(2)}) collective-permute-start(bf16[128,2048]{0,1:T(8,128)(2,1)S(1)} %copy.11), channel_id=1, source_target_pairs={{0,4},{1,5},{2,6},{3,7},{4,8},{5,9},{6,10},{7,11},{8,12},{9,13},{1... | collective-permute-start | bytes 1572872 | tf_op jit(solution)/shard_map/ppermute | solution.py:16
  21.5 13.9 %collective-permute-start.1 = (bf16[128,2048]{0,1:T(8,128)(2,1)S(1)}, bf16[128,2048]{0,1:T(8,128)(2,1)S(1)}, u32[]{:S(2)}, u32[]{:S(2)}) collective-permute-start(bf16[128,2048]{0,1:T(8,128)(2,1)S(1)} %copy.11), channel_id=1, source_target_pairs={{0,3},{1,4},{2,5},{3,6},{4,7},{5,8},{6,9},{7,10},{8,11},{9,12},{10... | collective-permute-start | bytes 1572872 | tf_op jit(solution)/shard_map/ppermute | solution.py:16
  24.5 22.1 %collective-permute-start.2 = (bf16[128,2048]{0,1:T(8,128)(2,1)S(1)}, bf16[128,2048]{0,1:T(8,128)(2,1)S(1)}, u32[]{:S(2)}, u32[]{:S(2)}) collective-permute-start(bf16[128,2048]{0,1:T(8,128)(2,1)S(1)} %copy.11), channel_id=1, source_target_pairs={{0,2},{1,3},{2,4},{3,5},{4,6},{5,7},{6,8},{7,9},{8,10},{9,11},{10,... | collective-permute-start | bytes 1572872 | tf_op jit(solution)/shard_map/ppermute | solution.py:16
  27.4 19.4 %collective-permute-start.3 = (bf16[128,2048]{0,1:T(8,128)(2,1)S(1)}, bf16[128,2048]{0,1:T(8,128)(2,1)S(1)}, u32[]{:S(2)}, u32[]{:S(2)}) collective-permute-start(bf16[128,2048]{0,1:T(8,128)(2,1)S(1)} %copy.11), channel_id=1, source_target_pairs={{0,1},{1,2},{2,3},{3,4},{4,5},{5,6},{6,7},{7,8},{8,9},{9,10},{10,1... | collective-permute-start | bytes 1572872 | tf_op jit(solution)/shard_map/ppermute | solution.py:16
  47.0 1.5 copy-start
  48.5 6.0 %copy-start.1 = (pred[128,640]{0,1:T(8,128)(4,1)S(1)}, pred[128,640]{0,1:T(8,128)(4,1)}, u32[]{:S(2)}) copy-start(pred[128,640]{0,1:T(8,128)(4,1)} %fusion.12) | copy-start | bytes 245764
  60.2 23.4 %copy-start.3 = (s32[1,2]{1,0:T(1,128)S(1)}, s32[1,2]{1,0:T(1,128)}, u32[]{:S(2)}) copy-start(s32[1,2]{1,0:T(1,128)} %param.8) | copy-start | bytes 28
  68.0 100.4 %collective-permute-start.8 = (bf16[128,8192]{0,1:T(8,128)(2,1)}, bf16[128,8192]{0,1:T(8,128)(2,1)}, u32[]{:S(2)}, u32[]{:S(2)}) collective-permute-start(bf16[128,8192]{0,1:T(8,128)(2,1)} %bitcast.60), channel_id=1, source_target_pairs={{0,8},{1,9},{2,10},{3,11},{4,12},{5,13},{6,14},{7,15},{8,0},{9,1},... | collective-permute-start | bytes 6291464 | tf_op jit(solution)/shard_map/ppermute | solution.py:63
